TPU v7x, 32 devices: a whole 2x2x4 slice. The times are simulated.
32 devices in a mesh: fsdp: 4 (over z), ctx: 8 (over y, x, core).
Axes of the slice: x: 2, y: 2, z: 4, core: 2. Of those that a mesh axis runs over, the one named last changes fastest.
Arguments:
- inputs: bfloat16 [24, 1024, 768], P('fsdp', 'ctx'), may hold values from -6 to 6
- cotangent: float32 [24, 1024, 768], P('fsdp', 'ctx'), may hold values from -6 to 6
- ln1_gain: bfloat16 [768], P(('fsdp', 'ctx')), may hold values from 0.5 to 1.5
- ln1_bias: bfloat16 [768], P(('fsdp', 'ctx')), may hold values from -1.25 to 1.25
- ln2_gain: bfloat16 [768], P(('fsdp', 'ctx')), may hold values from 0.5 to 1.5
- ln2_bias: bfloat16 [768], P(('fsdp', 'ctx')), may hold values from -1.25 to 1.25
- w_qkv: bfloat16 [768, 2304], P(('fsdp', 'ctx')), as said below
- b_qkv: bfloat16 [2304], P(('fsdp', 'ctx')), may hold values from -1.75 to 1.75
- w_out: bfloat16 [768, 768], P(('fsdp', 'ctx')), may hold values from -2.5 to 2.5
- b_out: bfloat16 [768], P(('fsdp', 'ctx')), may hold values from -1.75 to 1.75
- w_in: bfloat16 [768, 3072], P(('fsdp', 'ctx')), may hold values from -0.21875 to 0.21875
- b_in: bfloat16 [3072], P(('fsdp', 'ctx')), may hold values from -1.75 to 1.75
- w_mlp_out: bfloat16 [3072, 768], P(('fsdp', 'ctx')), may hold values from -0.109375 to 0.109375
- b_mlp_out: bfloat16 [768], P(('fsdp', 'ctx')), may hold values from -1.75 to 1.75
Outputs:
- outputs: float32 [24, 1024, 768], P('fsdp', 'ctx')
- grad_inputs: float32 [24, 1024, 768], P('fsdp', 'ctx')
- grad_ln1_gain: float32 [768], P(('fsdp', 'ctx'))
- grad_ln1_bias: float32 [768], P(('fsdp', 'ctx'))
- grad_ln2_gain: float32 [768], P(('fsdp', 'ctx'))
- grad_ln2_bias: float32 [768], P(('fsdp', 'ctx'))
- grad_w_qkv: float32 [768, 2304], P(('fsdp', 'ctx'))
- grad_b_qkv: float32 [2304], P(('fsdp', 'ctx'))
- grad_w_out: float32 [768, 768], P(('fsdp', 'ctx'))
- grad_b_out: float32 [768], P(('fsdp', 'ctx'))
- grad_w_in: float32 [768, 3072], P(('fsdp', 'ctx'))
- grad_b_in: float32 [3072], P(('fsdp', 'ctx'))
- grad_w_mlp_out: float32 [3072, 768], P(('fsdp', 'ctx'))
- grad_b_mlp_out: float32 [768], P(('fsdp', 'ctx'))
Inputs may be any that keep to these rules, and one draw needn't show every extreme that they name: `w_qkv`: a weight matrix whose entries lie within 24 / sqrt(768) of zero.
All inputs are finite; a program needn't handle non-finite values.
Results may differ from a plain program's by a relative error of at most 0.012.
Values may be sent and summed in bfloat16 or wider, within the bound.
No kernel may reach another device: no remote copies, remote signals or barrier semaphores. Data moves between devices by JAX's collectives and lax.ppermute only.
A program may use at most 448 MiB of HBM per device.

v0:
```python
import math
import jax
import jax.numpy as jnp
from jax import lax
from jax.sharding import PartitionSpec as P

HEADS = 12
HEAD_DIM = 64
ROT_DIM = 16
MICRO = 2
SEQ_MB = 3
EPS = 1e-05
BASE_FREQ = 10000.0


def layer_norm(values, gain_row, shift_row):
    centre = jnp.mean(values, axis=-1, keepdims=True)
    centred = values - centre
    inverse = lax.rsqrt(jnp.mean(centred * centred, axis=-1, keepdims=True) + EPS)
    normed = centred * inverse
    return (normed * gain_row + shift_row, normed, inverse)


def norm_back(grad_out, normed, inverse, gain_row):
    scaled = grad_out * gain_row
    return inverse * (
        scaled
        - jnp.mean(scaled, axis=-1, keepdims=True)
        - normed * jnp.mean(scaled * normed, axis=-1, keepdims=True)
    )


def angles(positions):
    half_rot = ROT_DIM // 2
    inv_freq = BASE_FREQ ** (-(2.0 * jnp.arange(half_rot, dtype=jnp.float32)) / ROT_DIM)
    phase_angle = positions.astype(jnp.float32)[:, None] * inv_freq[None, :]
    return (jnp.cos(phase_angle), jnp.sin(phase_angle))


def rotate(head_field, cosine, sine_rot, direction):
    half_rot = ROT_DIM // 2
    lead_half = head_field[..., :half_rot]
    trail_half = head_field[..., half_rot:ROT_DIM]
    cos_wide = cosine[:, None, :]
    sin_wide = direction * sine_rot[:, None, :]
    return jnp.concatenate(
        [
            lead_half * cos_wide - trail_half * sin_wide,
            trail_half * cos_wide + lead_half * sin_wide,
            head_field[..., ROT_DIM:],
        ],
        axis=-1,
    )


def gelu_parts(pre_act):
    normal_cdf = 0.5 * (1.0 + jax.scipy.special.erf(pre_act * 0.7071067811865476))
    density = jnp.exp(-0.5 * pre_act * pre_act) * 0.3989422804014327
    return (pre_act * normal_cdf, normal_cdf + pre_act * density)


def outer_rows(left, right):
    return lax.dot_general(
        left, right, (((0,), (0,)), ((), ())), preferred_element_type=jnp.float32
    )


def times_transpose(left, right):
    return lax.dot_general(
        left, right, (((1,), (1,)), ((), ())), preferred_element_type=jnp.float32
    )


def attend_block(soft_state, kv_block, first_row, query_low, positions, score_scale):
    run_max, run_sum, weighted = soft_state
    seq_count, block_rows, double_width = kv_block.shape
    model_width = double_width // 2
    key_low = kv_block[..., :model_width].reshape(seq_count, block_rows, HEADS, HEAD_DIM)
    value_low = kv_block[..., model_width:].reshape(seq_count, block_rows, HEADS, HEAD_DIM)
    scores = (
        jnp.einsum("sqhd,skhd->shqk", query_low, key_low, preferred_element_type=jnp.float32)
        * score_scale
    )
    allowed = (first_row + jnp.arange(block_rows, dtype=jnp.int32))[None, :] <= positions[:, None]
    scores = jnp.where(allowed, scores, -jnp.inf)
    new_max = jnp.maximum(run_max, jnp.max(scores, axis=-1))
    safe_max = jnp.where(new_max == -jnp.inf, 0.0, new_max)
    exp_scores = jnp.exp(scores - safe_max[..., None])
    factor = jnp.exp(run_max - safe_max)
    run_sum = run_sum * factor + jnp.sum(exp_scores, axis=-1)
    weighted = weighted * factor[..., None] + jnp.einsum(
        "shqk,skhd->shqd",
        exp_scores.astype(jnp.bfloat16),
        value_low,
        preferred_element_type=jnp.float32,
    )
    return (new_max, run_sum, weighted)


def attend_piece(soft_state, kv_piece, query_low, positions, score_scale):
    piece_rows = kv_piece.shape[1]
    step_rows = math.gcd(piece_rows, 512)

    def one_block(block_index, inner_state):
        offset = block_index * step_rows
        kv_block = lax.dynamic_slice_in_dim(kv_piece, offset, step_rows, 1)
        return attend_block(inner_state, kv_block, offset, query_low, positions, score_scale)

    return lax.fori_loop(0, piece_rows // step_rows, one_block, soft_state)


def local(
    inputs,
    cotangent,
    ln1_gain,
    ln1_bias,
    ln2_gain,
    ln2_bias,
    w_qkv,
    b_qkv,
    w_out,
    b_out,
    w_in,
    b_in,
    w_mlp_out,
    b_mlp_out,
):
    f32 = jnp.float32
    bf16 = jnp.bfloat16
    group_rows = inputs.shape[1]
    model_width = inputs.shape[2]
    seq_len = group_rows * lax.axis_size("ctx")
    key_block = math.gcd(seq_len, 512)
    score_scale = HEAD_DIM ** (-0.5)
    positions = lax.axis_index("ctx") * group_rows + jnp.arange(group_rows, dtype=jnp.int32)
    cosine, sine_rot = angles(positions)

    def gather_params():
        return (
            lax.all_gather(ln1_gain, ("fsdp", "ctx"), axis=0, tiled=True),
            lax.all_gather(ln1_bias, ("fsdp", "ctx"), axis=0, tiled=True),
            lax.all_gather(ln2_gain, ("fsdp", "ctx"), axis=0, tiled=True),
            lax.all_gather(ln2_bias, ("fsdp", "ctx"), axis=0, tiled=True),
            lax.all_gather(w_qkv, ("fsdp", "ctx"), axis=0, tiled=True),
            lax.all_gather(b_qkv, ("fsdp", "ctx"), axis=0, tiled=True),
            lax.all_gather(w_out, ("fsdp", "ctx"), axis=0, tiled=True),
            lax.all_gather(b_out, ("fsdp", "ctx"), axis=0, tiled=True),
            lax.all_gather(w_in, ("fsdp", "ctx"), axis=0, tiled=True),
            lax.all_gather(b_in, ("fsdp", "ctx"), axis=0, tiled=True),
            lax.all_gather(w_mlp_out, ("fsdp", "ctx"), axis=0, tiled=True),
            lax.all_gather(b_mlp_out, ("fsdp", "ctx"), axis=0, tiled=True),
        )

    weight_sums = None
    output_list = []
    grad_list = []
    for micro_index in range(MICRO):
        batch_rows = inputs[micro_index * SEQ_MB : (micro_index + 1) * SEQ_MB]
        cot_rows = cotangent[micro_index * SEQ_MB : (micro_index + 1) * SEQ_MB]
        seq_count = batch_rows.shape[0]
        flat_rows = seq_count * group_rows
        params_fwd = gather_params()
        (
            gain_one,
            shift_one,
            gain_two,
            shift_two,
            weight_qkv,
            bias_qkv,
            weight_out,
            bias_out,
            weight_in,
            bias_in,
            weight_mlp,
            bias_mlp,
        ) = params_fwd
        residual = batch_rows.reshape(flat_rows, model_width).astype(f32)
        normal_one, normed_one, inverse_one = layer_norm(
            residual, gain_one.astype(f32), shift_one.astype(f32)
        )
        normal_two, normed_two, inverse_two = layer_norm(
            residual, gain_two.astype(f32), shift_two.astype(f32)
        )
        hidden_one = normal_one.astype(bf16)
        hidden_two = normal_two.astype(bf16)
        project = jnp.dot(hidden_one, weight_qkv, preferred_element_type=f32) + bias_qkv.astype(f32)
        head_shape = (seq_count, group_rows, HEADS, HEAD_DIM)
        query_low = rotate(
            project[:, :model_width].reshape(head_shape), cosine, sine_rot, 1.0
        ).astype(bf16)
        key_low = rotate(
            project[:, model_width : 2 * model_width].reshape(head_shape), cosine, sine_rot, 1.0
        ).astype(bf16)
        value_low = project[:, 2 * model_width :].astype(bf16)
        kv_pack = jnp.concatenate(
            [
                key_low.reshape(seq_count, group_rows, model_width),
                value_low.reshape(seq_count, group_rows, model_width),
            ],
            axis=-1,
        )
        start_state = (
            jnp.full((seq_count, HEADS, group_rows), -jnp.inf, f32),
            jnp.zeros((seq_count, HEADS, group_rows), f32),
            jnp.zeros((seq_count, HEADS, group_rows, HEAD_DIM), f32),
        )
        soft_state = attend_piece(
            start_state,
            lax.all_gather(kv_pack, "ctx", axis=1, tiled=True),
            query_low,
            positions,
            score_scale,
        )
        run_max, run_sum, weighted = soft_state
        log_total = run_max + jnp.log(run_sum)
        attended = jnp.transpose(weighted / run_sum[..., None], (0, 2, 1, 3)).astype(bf16)
        att_flat = attended.reshape(flat_rows, model_width)
        pre_act = jnp.dot(hidden_two, weight_in, preferred_element_type=f32) + bias_in.astype(f32)
        activation_f, gelu_slope = gelu_parts(pre_act)
        activation = activation_f.astype(bf16)
        output = (
            residual
            + jnp.dot(att_flat, weight_out, preferred_element_type=f32)
            + bias_out.astype(f32)
            + jnp.dot(activation, weight_mlp, preferred_element_type=f32)
            + bias_mlp.astype(f32)
        )
        output_list.append(output.reshape(seq_count, group_rows, model_width))
        params_back = gather_params()
        (
            gain_one,
            shift_one,
            gain_two,
            shift_two,
            weight_qkv,
            bias_qkv,
            weight_out,
            bias_out,
            weight_in,
            bias_in,
            weight_mlp,
            bias_mlp,
        ) = params_back
        kv_rows = lax.all_gather(kv_pack, "ctx", axis=1, tiled=True)
        cot_flat = cot_rows.reshape(flat_rows, model_width)
        cot_low = cot_flat.astype(bf16)
        cot_sum = jnp.sum(cot_flat, axis=0)
        grad_w_out = outer_rows(att_flat, cot_low)
        grad_w_mlp = outer_rows(activation, cot_low)
        d_pre = times_transpose(cot_low, weight_mlp) * gelu_slope
        d_pre_low = d_pre.astype(bf16)
        grad_w_in = outer_rows(hidden_two, d_pre_low)
        d_hidden_two = times_transpose(d_pre_low, weight_in)
        grad_att = times_transpose(cot_low, weight_out).astype(bf16).reshape(head_shape)
        row_delta = jnp.einsum("sqhd,sqhd->shq", grad_att, attended, preferred_element_type=f32)

        def back_block(block_index, loop_carry):
            grad_query, buffer = loop_carry
            offset = block_index * key_block
            kv_block = lax.dynamic_slice_in_dim(kv_rows, offset, key_block, 1)
            key_part = kv_block[..., :model_width].reshape(seq_count, key_block, HEADS, HEAD_DIM)
            value_part = kv_block[..., model_width:].reshape(seq_count, key_block, HEADS, HEAD_DIM)
            scores = (
                jnp.einsum("sqhd,skhd->shqk", query_low, key_part, preferred_element_type=f32)
                * score_scale
            )
            allowed = (offset + jnp.arange(key_block, dtype=jnp.int32))[None, :] <= positions[
                :, None
            ]
            prob_block = jnp.where(allowed, jnp.exp(scores - log_total[..., None]), 0.0)
            grad_value = jnp.einsum(
                "shqk,sqhd->skhd", prob_block.astype(bf16), grad_att, preferred_element_type=f32
            )
            grad_prob = jnp.einsum(
                "sqhd,skhd->shqk", grad_att, value_part, preferred_element_type=f32
            )
            grad_score = (prob_block * (grad_prob - row_delta[..., None]) * score_scale).astype(
                bf16
            )
            grad_query = grad_query + jnp.einsum(
                "shqk,skhd->sqhd", grad_score, key_part, preferred_element_type=f32
            )
            grad_key = jnp.einsum(
                "shqk,sqhd->skhd", grad_score, query_low, preferred_element_type=f32
            )
            key_value_grad = jnp.concatenate(
                [
                    grad_key.reshape(seq_count, key_block, model_width),
                    grad_value.reshape(seq_count, key_block, model_width),
                ],
                axis=-1,
            )
            return (grad_query, lax.dynamic_update_slice_in_dim(buffer, key_value_grad, offset, 1))

        start_carry = (
            jnp.zeros(head_shape, f32),
            jnp.zeros((seq_count, seq_len, 2 * model_width), f32),
        )
        grad_query, buffer = lax.fori_loop(0, seq_len // key_block, back_block, start_carry)
        kv_grad_own = lax.psum_scatter(
            buffer.astype(jnp.bfloat16), "ctx", scatter_dimension=1, tiled=True
        ).astype(jnp.float32)
        key_grad_raw = kv_grad_own[..., :model_width].reshape(head_shape)
        value_grad_flat = kv_grad_own[..., model_width:].reshape(flat_rows, model_width)
        grad_query = rotate(grad_query, cosine, sine_rot, -1.0)
        grad_key = rotate(key_grad_raw, cosine, sine_rot, -1.0)
        d_project = jnp.concatenate(
            [
                grad_query.reshape(flat_rows, model_width),
                grad_key.reshape(flat_rows, model_width),
                value_grad_flat,
            ],
            axis=-1,
        )
        d_project_low = d_project.astype(bf16)
        grad_w_qkv = outer_rows(hidden_one, d_project_low)
        d_hidden_one = times_transpose(d_project_low, weight_qkv)
        grad_rows = (
            cot_flat
            + norm_back(d_hidden_one, normed_one, inverse_one, gain_one.astype(f32))
            + norm_back(d_hidden_two, normed_two, inverse_two, gain_two.astype(f32))
        )
        grad_list.append(grad_rows.reshape(seq_count, group_rows, model_width))
        terms = (
            jnp.sum(d_hidden_one * normed_one, axis=0),
            jnp.sum(d_hidden_one, axis=0),
            jnp.sum(d_hidden_two * normed_two, axis=0),
            jnp.sum(d_hidden_two, axis=0),
            grad_w_qkv,
            jnp.sum(d_project, axis=0),
            grad_w_out,
            cot_sum,
            grad_w_in,
            jnp.sum(d_pre, axis=0),
            grad_w_mlp,
            cot_sum,
        )
        if weight_sums is None:
            weight_sums = terms
        else:
            weight_sums = jax.tree.map(lambda total, term: total + term, weight_sums, terms)
    owned = (
        lax.psum_scatter(weight_sums[0], ("fsdp", "ctx"), scatter_dimension=0, tiled=True),
        lax.psum_scatter(weight_sums[1], ("fsdp", "ctx"), scatter_dimension=0, tiled=True),
        lax.psum_scatter(weight_sums[2], ("fsdp", "ctx"), scatter_dimension=0, tiled=True),
        lax.psum_scatter(weight_sums[3], ("fsdp", "ctx"), scatter_dimension=0, tiled=True),
        lax.psum_scatter(weight_sums[4], ("fsdp", "ctx"), scatter_dimension=0, tiled=True),
        lax.psum_scatter(weight_sums[5], ("fsdp", "ctx"), scatter_dimension=0, tiled=True),
        lax.psum_scatter(weight_sums[6], ("fsdp", "ctx"), scatter_dimension=0, tiled=True),
        lax.psum_scatter(weight_sums[7], ("fsdp", "ctx"), scatter_dimension=0, tiled=True),
        lax.psum_scatter(weight_sums[8], ("fsdp", "ctx"), scatter_dimension=0, tiled=True),
        lax.psum_scatter(weight_sums[9], ("fsdp", "ctx"), scatter_dimension=0, tiled=True),
        lax.psum_scatter(weight_sums[10], ("fsdp", "ctx"), scatter_dimension=0, tiled=True),
        lax.psum_scatter(weight_sums[11], ("fsdp", "ctx"), scatter_dimension=0, tiled=True),
    )
    outputs = jnp.concatenate(output_list, axis=0)
    grad_inputs = jnp.concatenate(grad_list, axis=0)
    return (
        outputs,
        grad_inputs,
        owned[0],
        owned[1],
        owned[2],
        owned[3],
        owned[4],
        owned[5],
        owned[6],
        owned[7],
        owned[8],
        owned[9],
        owned[10],
        owned[11],
    )


def solution(mesh):
    return jax.shard_map(
        local,
        mesh=mesh,
        in_specs=(
            P("fsdp", "ctx", None),
            P("fsdp", "ctx", None),
            P(("fsdp", "ctx")),
            P(("fsdp", "ctx")),
            P(("fsdp", "ctx")),
            P(("fsdp", "ctx")),
            P(("fsdp", "ctx"), None),
            P(("fsdp", "ctx")),
            P(("fsdp", "ctx"), None),
            P(("fsdp", "ctx")),
            P(("fsdp", "ctx"), None),
            P(("fsdp", "ctx")),
            P(("fsdp", "ctx"), None),
            P(("fsdp", "ctx")),
        ),
        out_specs=(
            P("fsdp", "ctx", None),
            P("fsdp", "ctx", None),
            P(("fsdp", "ctx")),
            P(("fsdp", "ctx")),
            P(("fsdp", "ctx")),
            P(("fsdp", "ctx")),
            P(("fsdp", "ctx"), None),
            P(("fsdp", "ctx")),
            P(("fsdp", "ctx"), None),
            P(("fsdp", "ctx")),
            P(("fsdp", "ctx"), None),
            P(("fsdp", "ctx")),
            P(("fsdp", "ctx"), None),
            P(("fsdp", "ctx")),
        ),
        check_vma=False,
    )
```

profile of v0, /device:TPU:0, one launch (start us, length us, event | category | flops | bytes accessed | tf_op | source)
XLA Modules:
  0.0 1064.9 jit_solution(9018735017955234770)
XLA Ops:
  15.5 42.9 %all-reduce.16 = (bf16[768]{0:T(1024)(128)(2,1)S(1)}, bf16[768]{0:T(1024)(128)(2,1)S(1)}, bf16[3072]{0:T(1024)(128)(2,1)}, bf16[768]{0:T(1024)(128)(2,1)}, bf16[...) all-reduce(bf16[768]{0:T(1024)(128)(2,1)S(1)} %dynamic-update-slice, ...), channel_id=1, replica_groups=mesh['fsdp'=4,'ctx'=8] {'fsdp','ctx'}, use_global_device_ids=true, to_apply=%add.5 | all-reduce | flops 9984 | bytes 39936
  64.4 9.1 all-gather.7.cloned.1.call-done
  108.7 20.5 %all-gather.11.cloned.1.call-done = bf16[768,768]{1,0:T(8,128)(2,1)} async-done(((bf16[24,768]{1,0:T(8,128)(2,1)}), bf16[768,768]{1,0:T(8,128)(2,1)}) %all-gather.11.cloned.1.call-update) | async-done | bytes 1179664 | tf_op jit(solution)/shard_map/all_gather | solution.py:146
  142.9 47.7 %all-gather.9.cloned.1.call-done = bf16[3,1024,1536]{1,2,0:T(8,128)(2,1)} async-done(((bf16[3,128,1536]{1,2,0:T(8,128)(2,1)}), bf16[3,1024,1536]{1,2,0:T(8,128)(2,1)}) %all-gather.9.cloned.1.call-update) | async-done | bytes 9437200 | tf_op jit(solution)/shard_map/all_gather | solution.py:209
  190.5 39.3 %while.68 = (s32[]{:T(128)}, f32[3,12,128]{2,1,0:T(8,128)S(1)}, f32[3,12,128]{2,1,0:T(8,128)S(1)}, f32[3,12,128,64]{2,3,1,0:T(8,128)}, bf16[3,1024,1536]{1,2,0:T...) while((s32[]{:T(128)}, f32[3,12,128]{2,1,0:T(8,128)S(1)}, ...), condition=%wide.region_5.0_spmd.clone, body=%wide.region_2.5_spmd.clone.sunk | while | flops 630924416 | bytes 83746024 | solution.py:109
  198.4 6.6 fusion.242
  217.3 5.9 fusion.242
  224.8 5.0 fusion.244
  238.3 62.6 %while.70 = (s32[]{:T(128)}, f32[3,128,12,64]{1,3,2,0:T(8,128)}, bf16[3,1024,1536]{2,1,0:T(8,128)(2,1)}, bf16[3,1024,1536]{1,2,0:T(8,128)(2,1)}, bf16[3,128,12,6...) while((s32[]{:T(128)}, f32[3,128,12,64]{1,3,2,0:T(8,128)}, ...), condition=%wide.region_13.14_spmd.clone, body=%wide.region_12.13_spmd.clone.sunk | while | flops 1545994880 | bytes 116010296 | solution.py:299
  253.9 6.6 copy.224
  284.8 6.6 copy.224
  291.4 4.8 constant_dynamic-update-slice_fusion.4
  302.0 37.5 %while.69 = (s32[]{:T(128)}, f32[3,12,128]{2,1,0:T(8,128)S(1)}, f32[3,12,128]{2,1,0:T(8,128)S(1)}, f32[3,12,128,64]{2,3,1,0:T(8,128)}, bf16[3,1024,1536]{1,2,0:T...) while((s32[]{:T(128)}, f32[3,12,128]{2,1,0:T(8,128)S(1)}, ...), condition=%wide.region_11.12_spmd.clone, body=%wide.region_8.0_spmd.clone.sunk | while | flops 630924416 | bytes 83746024 | solution.py:109
  310.1 6.0 fusion.250
  328.1 5.9 fusion.250
  334.6 4.9 fusion.252
  348.0 64.4 %while.71 = (s32[]{:T(128)}, f32[3,128,12,64]{1,3,2,0:T(8,128)}, bf16[3,1024,1536]{2,1,0:T(8,128)(2,1)}, bf16[3,1024,1536]{1,2,0:T(8,128)(2,1)}, bf16[3,128,12,6...) while((s32[]{:T(128)}, f32[3,128,12,64]{1,3,2,0:T(8,128)}, ...), condition=%wide.region_20.21_spmd.clone, body=%wide.region_19.20_spmd.clone.sunk | while | flops 1545994880 | bytes 116010296 | solution.py:299
  363.4 6.8 copy.225
  395.4 7.2 copy.225
  402.6 5.0 constant_dynamic-update-slice_fusion.5
  413.5 7.1 multiply_convert_fusion.1
  420.6 6.5 fusion.118
  439.1 5.2 convolution_add_fusion.2
  448.7 5.2 convolution_add_fusion.1
  470.4 72.2 %reduce-scatter.9.cloned.1.call-done = bf16[3,128,1536]{2,1,0:T(8,128)(2,1)} async-done(((bf16[3,1024,1536]{2,1,0:T(8,128)(2,1)}), bf16[3,128,1536]{2,1,0:T(8,128)(2,1)}) %reduce-scatter.9.cloned.1.call-update) | async-done | bytes 1179664 | tf_op jit(solution)/shard_map/reduce_scatter | solution.py:300
  568.0 5.0 convolution_add_fusion
  575.3 5.1 fusion.91
  601.6 42.3 %all-reduce.15 = (f32[768]{0:T(1024)S(1)}, f32[768]{0:T(1024)S(1)}, f32[768]{0:T(1024)S(1)}, f32[768]{0:T(1024)S(1)}, f32[2304]{0:T(1024)S(1)}, /*index=5*/f32[768]{0:T(1024)S(1)}, f32[3072]{0:T(1024)S(1)}) all-reduce(f32[768]{0:T(1024)S(1)} %add.485, f32[768]{0:T(1024)S(1)} %add.486, ...), channel_id=4, replica_groups=mesh['fsdp'=4,'ctx'=8] {'fsdp','ctx'}, use_global_device_ids=true, to_apply=%region_28.29.clone | all-reduce | flops 9216 | bytes 73728
  657.9 28.6 %reduce-scatter.15.cloned.1.call-done = f32[24,3072]{1,0:T(8,128)} async-done(((f32[768,3072]{1,0:T(8,128)}), f32[24,3072]{1,0:T(8,128)}) %reduce-scatter.15.cloned.1.call-update) | async-done | bytes 294928 | tf_op jit(solution)/shard_map/reduce_scatter | solution.py:351
  686.5 141.5 %reduce-scatter.17.cloned.1.call-done = f32[96,768]{1,0:T(8,128)} async-done(((f32[3072,768]{1,0:T(8,128)}), f32[96,768]{1,0:T(8,128)}) %reduce-scatter.17.cloned.1.call-update) | async-done | bytes 294928 | tf_op jit(solution)/shard_map/reduce_scatter | solution.py:353
  828.0 104.4 %reduce-scatter.13.cloned.1.call-done = f32[24,768]{1,0:T(8,128)} async-done(((f32[768,768]{1,0:T(8,128)}), f32[24,768]{1,0:T(8,128)}) %reduce-scatter.13.cloned.1.call-update) | async-done | bytes 73744 | tf_op jit(solution)/shard_map/reduce_scatter | solution.py:349
  932.3 124.8 %reduce-scatter.11.cloned.1.call-done = f32[24,2304]{1,0:T(8,128)} async-done(((f32[768,2304]{1,0:T(8,128)}), f32[24,2304]{1,0:T(8,128)}) %reduce-scatter.11.cloned.1.call-update) | async-done | bytes 221200 | tf_op jit(solution)/shard_map/reduce_scatter | solution.py:347
  (499 shorter events, 308.0 us)
Async XLA Ops:
  7.2 54.5 %copy-start.7 = (bf16[6,128,768]{2,1,0:T(8,128)(2,1)S(1)}, bf16[6,128,768]{2,1,0:T(8,128)(2,1)}, u32[]{:S(2)}) copy-start(bf16[6,128,768]{2,1,0:T(8,128)(2,1)} %param.22) | copy-start | bytes 3538948
  7.2 66.4 %all-gather.7.cloned.1.call-start = ((), (), s32[]{:S(2)}) async-start(), calls=%async_computation.6 | async-start | bytes 3649536 | tf_op jit(solution)/shard_map/all_gather | solution.py:144
  7.9 121.3 %all-gather.11.cloned.1.call-start = ((), (), s32[]{:S(2)}) async-start(), calls=%async_computation.8 | async-start | bytes 1216512 | tf_op jit(solution)/shard_map/all_gather | solution.py:146
  8.7 181.9 %all-gather.9.cloned.1.call-start = ((), (), s32[]{:S(2)}) async-start(), calls=%async_computation.7 | async-start | bytes 10616832 | tf_op jit(solution)/shard_map/all_gather | solution.py:209
  61.6 15.5 %copy-start.80 = (f32[384]{0:T(512)}, f32[384]{0:T(512)S(1)}, u32[]{:S(2)}) copy-start(f32[384]{0:T(512)S(1)} %rsqrt_bitcast_fusion) | copy-start | bytes 4612
  61.7 15.5 %copy-start.78 = (f32[384]{0:T(512)}, f32[384]{0:T(512)S(1)}, u32[]{:S(2)}) copy-start(f32[384]{0:T(512)S(1)} %rsqrt_bitcast_fusion.1) | copy-start | bytes 4612
  63.6 13.5 %copy-start.43 = (bf16[384,768]{1,0:T(8,128)(2,1)}, bf16[384,768]{1,0:T(8,128)(2,1)S(1)}, u32[]{:S(2)}) copy-start(bf16[384,768]{1,0:T(8,128)(2,1)S(1)} %get-tuple-element.948) | copy-start | bytes 1769476
  64.4 27.7 %copy-start.72 = (f32[128,8]{0,1:T(8,128)}, f32[128,8]{0,1:T(8,128)S(1)}, u32[]{:S(2)}) copy-start(f32[128,8]{0,1:T(8,128)S(1)} %get-tuple-element.973) | copy-start | bytes 12292
  64.4 12.7 %copy-start.90 = (f32[2304]{0:T(1024)}, f32[2304]{0:T(1024)S(1)}, u32[]{:S(2)}) copy-start(f32[2304]{0:T(1024)S(1)} %convert_element_type.201) | copy-start | bytes 27652
  96.9 204.1 %all-gather.17.cloned.1.call-start = ((), (), s32[]{:S(2)}) async-start(), calls=%async_computation.11 | async-start | bytes 10616832 | tf_op jit(solution)/shard_map/all_gather | solution.py:209
  103.9 309.1 %all-gather.13.cloned.1.call-start = ((), (), s32[]{:S(2)}) async-start(), calls=%async_computation.9 | async-start | bytes 4866048 | tf_op jit(solution)/shard_map/all_gather | solution.py:148
  104.5 316.1 %all-gather.15.cloned.1.call-start = ((), (), s32[]{:S(2)}) async-start(), calls=%async_computation.10 | async-start | bytes 4866048 | tf_op jit(solution)/shard_map/all_gather | solution.py:150
  105.1 362.0 %reduce-scatter.7.cloned.1.call-start = ((), (), s32[]{:S(2)}) async-start(), calls=%async_computation.12 | async-start | bytes 10616832 | tf_op jit(solution)/shard_map/reduce_scatter | solution.py:300
  108.7 22.5 %copy-start.45 = (bf16[384,768]{1,0:T(8,128)(2,1)}, bf16[384,768]{1,0:T(8,128)(2,1)S(1)}, u32[]{:S(2)}) copy-start(bf16[384,768]{1,0:T(8,128)(2,1)S(1)} %get-tuple-element.986) | copy-start | bytes 1769476
  198.4 7.4 copy-start
  217.3 7.5 copy-start
  301.0 241.6 %reduce-scatter.9.cloned.1.call-start = ((), (), s32[]{:S(2)}) async-start(), calls=%async_computation.13 | async-start | bytes 10616832 | tf_op jit(solution)/shard_map/reduce_scatter | solution.py:300
  310.1 6.5 copy-start.1
  412.4 274.1 %reduce-scatter.15.cloned.1.call-start = ((), (), s32[]{:S(2)}) async-start(), calls=%async_computation.16 | async-start | bytes 9732096 | tf_op jit(solution)/shard_map/reduce_scatter | solution.py:351
  413.5 7.1 copy-start.46
  427.1 6.5 slice-start.2
  433.6 15.1 %copy-start.23 = (bf16[384,3072]{1,0:T(8,128)(2,1)}, bf16[384,3072]{1,0:T(8,128)(2,1)S(1)}, u32[]{:S(2)}) copy-start(bf16[384,3072]{1,0:T(8,128)(2,1)S(1)} %get-tuple-element.974) | copy-start | bytes 7077892
  444.3 383.6 %reduce-scatter.17.cloned.1.call-start = ((), (), s32[]{:S(2)}) async-start(), calls=%async_computation.17 | async-start | bytes 9732096 | tf_op jit(solution)/shard_map/reduce_scatter | solution.py:353
  454.0 478.3 %reduce-scatter.13.cloned.1.call-start = ((), (), s32[]{:S(2)}) async-start(), calls=%async_computation.15 | async-start | bytes 2433024 | tf_op jit(solution)/shard_map/reduce_scatter | solution.py:349
  459.9 597.2 %reduce-scatter.11.cloned.1.call-start = ((), (), s32[]{:S(2)}) async-start(), calls=%async_computation.14 | async-start | bytes 7299072 | tf_op jit(solution)/shard_map/reduce_scatter | solution.py:347
  552.4 39.8 %copy-start.13 = (f32[96,8,3,128]{3,1,2,0:T(8,128)}, f32[96,8,3,128]{3,1,2,0:T(8,128)S(1)}, u32[]{:S(2)}) copy-start(f32[96,8,3,128]{3,1,2,0:T(8,128)S(1)} %copy.221) | copy-start | bytes 3538948
  552.9 11.7 %copy-start.15 = (f32[96,8,3,128]{3,1,2,0:T(8,128)}, f32[96,8,3,128]{3,1,2,0:T(8,128)S(1)}, u32[]{:S(2)}) copy-start(f32[96,8,3,128]{3,1,2,0:T(8,128)S(1)} %copy.220) | copy-start | bytes 3538948
  575.3 7.4 slice-start.4
  580.4 16.4 %copy-start.55 = (f32[384,768]{1,0:T(8,128)}, f32[384,768]{1,0:T(8,128)S(1)}, u32[]{:S(2)}) copy-start(f32[384,768]{1,0:T(8,128)S(1)} %fusion.91) | copy-start | bytes 3538948
  582.8 14.0 %copy-start.57 = (f32[384,768]{1,0:T(8,128)}, f32[384,768]{1,0:T(8,128)S(1)}, u32[]{:S(2)}) copy-start(f32[384,768]{1,0:T(8,128)S(1)} %fusion.87) | copy-start | bytes 3538948
  596.9 55.9 %copy-start.12 = (f32[3,128,768]{2,1,0:T(8,128)S(1)}, f32[3,128,768]{2,1,0:T(8,128)}, u32[]{:S(2)}) copy-start(f32[3,128,768]{2,1,0:T(8,128)} %copy-done.11) | copy-start | bytes 3538948
  644.0 413.2 %copy-start.99 = (f32[24]{0:T(128)}, f32[24]{0:T(128)S(1)}, u32[]{:S(2)}) copy-start(f32[24]{0:T(128)S(1)} %dynamic-slice.5) | copy-start | bytes 292
  (94 other events, 222.3 us)
Sparse Core Ops, SparseCore 0:
  10.9 62.6 all-gather.6
  76.5 52.7 all-gather.10
  131.1 59.3 all-gather.8
  192.3 60.4 all-gather.16
  255.5 63.6 all-gather.12
  322.0 61.9 all-gather.14
  387.4 74.9 reduce-scatter.6
  465.9 76.6 reduce-scatter.8
  549.0 137.3 reduce-scatter.14
  692.8 135.1 reduce-scatter.16
  833.8 98.4 reduce-scatter.12
  938.4 118.6 reduce-scatter.10
where the time goes:
time: 1080 us; the launch traced here: 1060 us
  waiting for transfers between devices  551 us (51%)
  matrix products  170 us (16%)
  local copies, waits for them, and re-layouts  158 us (15%)
  blocking collectives  85.2 us (8%)
  other arithmetic  81.9 us (8%)
  between operations  16.1 us (1%)
    reduce_scatter x1, waiting for transfers between devices, local(): lax.psum_scatter(weight_sums[10], ('fsdp', 'ctx'), scatter_dimension=0, t...  141 us
    reduce_scatter x1, waiting for transfers between devices, local(): lax.psum_scatter(weight_sums[4], ('fsdp', 'ctx'), scatter_dimension=0, ti...  125 us
    reduce_scatter x1, waiting for transfers between devices, local(): lax.psum_scatter(weight_sums[6], ('fsdp', 'ctx'), scatter_dimension=0, ti...  104 us
    unnamed x2, blocking collectives  85.2 us
    reduce_scatter x2, waiting for transfers between devices, local(): lax.psum_scatter(buffer.astype(jnp.bfloat16), 'ctx', scatter_dimension=1,...  72.2 us
    all_gather x2, waiting for transfers between devices, local(): lax.all_gather(kv_pack, 'ctx', axis=1, tiled=True)  47.7 us
    dynamic_update_slice x8, local copies, waits for them, and re-layouts, back_block(): lax.dynamic_update_slice_in_dim(buffer, key_value_grad, offset, 1)  46.6 us
    unnamed x228, local copies, waits for them, and re-layouts  31.5 us
  transfers between devices with their start and end apart: 12, of which 8 were waited for; matrix products, arithmetic and copies ran while one was open for 37% of the time, Pallas kernels for 0%

commit v1 on v0

--- a/solution.py
+++ b/solution.py
@@ -206,7 +206,9 @@
         )
         soft_state = attend_piece(
             start_state,
-            lax.all_gather(kv_pack, "ctx", axis=1, tiled=True),
+            jnp.concatenate(
+                lax.all_to_all(jnp.stack([kv_pack] * lax.axis_size("ctx")), "ctx", 0, 0), axis=1
+            ),
             query_low,
             positions,
             score_scale,

time: 1080 us -> 1220 us (1.13)
  local copies, waits for them, and re-layouts: 158 us -> 219 us
  waiting for transfers between devices: 551 us -> 609 us
  matrix products: 170 us -> 190 us
    all_to_all x0 -> x2, waiting for transfers between devices: none -> 167 us  [local(): lax.all_to_all(jnp.stack([kv_pack] * lax.axis_size('ctx')), 'ctx', 0, 0)]
    reduce_scatter x1, waiting for transfers between devices: 28.6 us -> 134 us  [local(): lax.psum_scatter(weight_sums[8], ('fsdp', 'ctx'), scatter_dimension=0, ti...]
    reduce_scatter x1, waiting for transfers between devices: 104 us -> 0.01 us  [local(): lax.psum_scatter(weight_sums[6], ('fsdp', 'ctx'), scatter_dimension=0, ti...]
    all_gather x2, waiting for transfers between devices: 47.7 us -> 0.01 us  [local(): kv_rows = lax.all_gather(kv_pack, 'ctx', axis=1, tiled=True)]
    reduce_scatter x2, waiting for transfers between devices: 72.2 us -> 30.1 us  [local(): lax.psum_scatter(buffer.astype(jnp.bfloat16), 'ctx', scatter_dimension=1,...]
    all_to_all x0 -> x2, local copies, waits for them, and re-layouts: none -> 25.4 us  [local(): lax.all_to_all(jnp.stack([kv_pack] * lax.axis_size('ctx')), 'ctx', 0, 0)]
    all_gather x1, waiting for transfers between devices: 20.5 us -> 0.02 us  [gather_params(): lax.all_gather(w_out, ('fsdp', 'ctx'), axis=0, tiled=True)]
    while x36 -> x44, local copies, waits for them, and re-layouts: 5.05 us -> 23.3 us
  transfers between devices with their start and end apart: 12 -> 14, of which waited for: 8 -> 7; matrix products, arithmetic and copies ran while one was open for 37% -> 39% of each run, Pallas kernels for 0% -> 0%
where the time goes in v1:
time: 1220 us; the launch traced here: 1210 us
  waiting for transfers between devices  609 us (50%)
  local copies, waits for them, and re-layouts  219 us (18%)
  matrix products  190 us (16%)
  blocking collectives  83.6 us (7%)
  other arithmetic  79.5 us (7%)
  between operations  16.2 us (1%)
    all_to_all x2, waiting for transfers between devices, local(): lax.all_to_all(jnp.stack([kv_pack] * lax.axis_size('ctx')), 'ctx', 0, 0)  167 us
    reduce_scatter x1, waiting for transfers between devices, local(): lax.psum_scatter(weight_sums[10], ('fsdp', 'ctx'), scatter_dimension=0, t...  142 us
    reduce_scatter x1, waiting for transfers between devices, local(): lax.psum_scatter(weight_sums[8], ('fsdp', 'ctx'), scatter_dimension=0, ti...  134 us
    reduce_scatter x1, waiting for transfers between devices, local(): lax.psum_scatter(weight_sums[4], ('fsdp', 'ctx'), scatter_dimension=0, ti...  125 us
    unnamed x2, blocking collectives  83.6 us
    dynamic_update_slice x8, local copies, waits for them, and re-layouts, back_block(): lax.dynamic_update_slice_in_dim(buffer, key_value_grad, offset, 1)  46.2 us
    dot_general x4, matrix products, attend_block(): jnp.einsum('shqk,skhd->shqd', exp_scores.astype(jnp.bfloat16), value_low,...  33 us
    unnamed x222, local copies, waits for them, and re-layouts  30.5 us
  transfers between devices with their start and end apart: 14, of which 7 were waited for; matrix products, arithmetic and copies ran while one was open for 39% of the time, Pallas kernels for 0%

profile of v1, /device:TPU:0, one launch (start us, length us, event | category | flops | bytes accessed | tf_op | source)
XLA Modules:
  0.0 1209.7 jit_solution(384002076512534675)
XLA Ops:
  15.5 42.9 %all-reduce.16 = (bf16[768]{0:T(1024)(128)(2,1)S(1)}, bf16[768]{0:T(1024)(128)(2,1)S(1)}, bf16[3072]{0:T(1024)(128)(2,1)}, bf16[768]{0:T(1024)(128)(2,1)}, bf16[...) all-reduce(bf16[768]{0:T(1024)(128)(2,1)S(1)} %dynamic-update-slice, ...), channel_id=1, replica_groups=mesh['fsdp'=4,'ctx'=8] {'fsdp','ctx'}, use_global_device_ids=true, to_apply=%add.5 | all-reduce | flops 9984 | bytes 39936
  64.4 9.2 all-gather.7.cloned.1.call-done
  102.0 5.6 stack.4
  116.7 125.5 %all-to-all-done = bf16[8,3,128,1536]{2,3,1,0:T(8,128)(2,1)} async-done(((bf16[8,3,128,1536]{2,3,1,0:T(8,128)(2,1)}), bf16[8,3,128,1536]{2,3,1,0:T(8,128)(2,1)}, u32[]{:S(2)}, u32[]{:S(2)}) %all-to-all-start) | async-done | bytes 9437216 | tf_op jit(solution)/shard_map/all_to_all | solution.py:210
  242.2 5.6 stack.5
  267.5 12.7 %copy.151 = bf16[8,3,128,1536]{3,2,0,1:T(8,128)(2,1)} copy(bf16[8,3,128,1536]{2,3,1,0:T(8,128)(2,1)} %all-to-all-done) | data formatting | bytes 18874368 | tf_op jit(solution)/shard_map/all_to_all | solution.py:210
  280.2 59.0 %while.68 = (s32[]{:T(128)}, f32[3,12,128]{2,1,0:T(8,128)S(1)}, f32[3,12,128]{2,1,0:T(8,128)S(1)}, f32[3,12,128,64]{2,3,1,0:T(8,128)}, bf16[3,1024,1536]{2,1,0:T...) while((s32[]{:T(128)}, f32[3,12,128]{2,1,0:T(8,128)S(1)}, ...), condition=%wide.region_5.0_spmd.clone, body=%wide.region_2.5_spmd.clone.sunk | while | flops 630924416 | bytes 64871652 | solution.py:109
  292.8 6.5 fusion.242
  301.8 8.1 fusion.244
  322.5 5.9 fusion.242
  330.8 8.4 fusion.244
  343.2 41.5 %all-to-all-done.1 = bf16[8,3,128,1536]{2,3,1,0:T(8,128)(2,1)} async-done(((bf16[8,3,128,1536]{2,3,1,0:T(8,128)(2,1)}), bf16[8,3,128,1536]{2,3,1,0:T(8,128)(2,1)}, u32[]{:S(2)}, u32[]{:S(2)}) %all-to-all-start.1) | async-done | bytes 9437216 | tf_op jit(solution)/shard_map/all_to_all | solution.py:210
  384.8 12.7 %copy.159 = bf16[8,3,128,1536]{3,2,0,1:T(8,128)(2,1)} copy(bf16[8,3,128,1536]{2,3,1,0:T(8,128)(2,1)} %all-to-all-done.1) | data formatting | bytes 18874368 | tf_op jit(solution)/shard_map/all_to_all | solution.py:210
  401.9 62.5 %while.70 = (s32[]{:T(128)}, f32[3,128,12,64]{1,3,2,0:T(8,128)}, bf16[3,1024,1536]{2,1,0:T(8,128)(2,1)}, bf16[3,1024,1536]{1,2,0:T(8,128)(2,1)}, bf16[3,128,12,6...) while((s32[]{:T(128)}, f32[3,128,12,64]{1,3,2,0:T(8,128)}, ...), condition=%wide.region_13.14_spmd.clone, body=%wide.region_12.13_spmd.clone.sunk | while | flops 1545994880 | bytes 116010296 | solution.py:301
  417.2 6.7 copy.284
  448.1 6.7 copy.284
  465.5 59.5 %while.69 = (s32[]{:T(128)}, f32[3,12,128]{2,1,0:T(8,128)S(1)}, f32[3,12,128]{2,1,0:T(8,128)S(1)}, f32[3,12,128,64]{2,3,1,0:T(8,128)}, bf16[3,1024,1536]{2,1,0:T...) while((s32[]{:T(128)}, f32[3,12,128]{2,1,0:T(8,128)S(1)}, ...), condition=%wide.region_11.12_spmd.clone, body=%wide.region_8.0_spmd.clone.sunk | while | flops 630924416 | bytes 64871652 | solution.py:109
  478.3 5.9 fusion.250
  486.7 8.1 fusion.252
  507.5 6.5 fusion.250
  516.5 8.5 fusion.252
  533.3 63.8 %while.71 = (s32[]{:T(128)}, f32[3,128,12,64]{1,3,2,0:T(8,128)}, bf16[3,1024,1536]{2,1,0:T(8,128)(2,1)}, bf16[3,1024,1536]{1,2,0:T(8,128)(2,1)}, bf16[3,128,12,6...) while((s32[]{:T(128)}, f32[3,128,12,64]{1,3,2,0:T(8,128)}, ...), condition=%wide.region_20.21_spmd.clone, body=%wide.region_19.20_spmd.clone.sunk | while | flops 1545994880 | bytes 116010296 | solution.py:301
  549.2 6.7 copy.285
  580.7 6.7 copy.285
  599.7 7.2 multiply_convert_fusion.1
  612.1 6.2 fusion.118
  621.1 6.1 multiply_convert_fusion
  658.5 30.1 %reduce-scatter.9.cloned.1.call-done = bf16[3,128,1536]{2,1,0:T(8,128)(2,1)} async-done(((bf16[3,1024,1536]{2,1,0:T(8,128)(2,1)}), bf16[3,128,1536]{2,1,0:T(8,128)(2,1)}) %reduce-scatter.9.cloned.1.call-update) | async-done | bytes 1179664 | tf_op jit(solution)/shard_map/reduce_scatter | solution.py:302
  746.9 40.7 %all-reduce.15 = (f32[768]{0:T(1024)S(1)}, f32[768]{0:T(1024)S(1)}, f32[768]{0:T(1024)S(1)}, f32[768]{0:T(1024)S(1)}, f32[2304]{0:T(1024)S(1)}, /*index=5*/f32[768]{0:T(1024)S(1)}, f32[3072]{0:T(1024)S(1)}) all-reduce(f32[768]{0:T(1024)S(1)} %add.485, f32[768]{0:T(1024)S(1)} %add.486, ...), channel_id=4, replica_groups=mesh['fsdp'=4,'ctx'=8] {'fsdp','ctx'}, use_global_device_ids=true, to_apply=%region_28.29.clone | all-reduce | flops 9216 | bytes 73728
  801.6 134.0 %reduce-scatter.15.cloned.1.call-done = f32[24,3072]{1,0:T(8,128)} async-done(((f32[768,3072]{1,0:T(8,128)}), f32[24,3072]{1,0:T(8,128)}) %reduce-scatter.15.cloned.1.call-update) | async-done | bytes 294928 | tf_op jit(solution)/shard_map/reduce_scatter | solution.py:353
  935.6 141.6 %reduce-scatter.17.cloned.1.call-done = f32[96,768]{1,0:T(8,128)} async-done(((f32[3072,768]{1,0:T(8,128)}), f32[96,768]{1,0:T(8,128)}) %reduce-scatter.17.cloned.1.call-update) | async-done | bytes 294928 | tf_op jit(solution)/shard_map/reduce_scatter | solution.py:355
  1077.2 124.6 %reduce-scatter.11.cloned.1.call-done = f32[24,2304]{1,0:T(8,128)} async-done(((f32[768,2304]{1,0:T(8,128)}), f32[24,2304]{1,0:T(8,128)}) %reduce-scatter.11.cloned.1.call-update) | async-done | bytes 221200 | tf_op jit(solution)/shard_map/reduce_scatter | solution.py:349
  (509 shorter events, 361.6 us)
Async XLA Ops:
  7.2 54.5 %copy-start.7 = (bf16[6,128,768]{2,1,0:T(8,128)(2,1)S(1)}, bf16[6,128,768]{2,1,0:T(8,128)(2,1)}, u32[]{:S(2)}) copy-start(bf16[6,128,768]{2,1,0:T(8,128)(2,1)} %param.22) | copy-start | bytes 3538948
  7.2 66.4 %all-gather.7.cloned.1.call-start = ((), (), s32[]{:S(2)}) async-start(), calls=%async_computation.8 | async-start | bytes 3649536 | tf_op jit(solution)/shard_map/all_gather | solution.py:144
  7.9 245.1 %all-gather.9.cloned.1.call-start = ((), (), s32[]{:S(2)}) async-start(), calls=%async_computation.9 | async-start | bytes 1216512 | tf_op jit(solution)/shard_map/all_gather | solution.py:146
  8.7 388.8 %all-gather.15.cloned.1.call-start = ((), (), s32[]{:S(2)}) async-start(), calls=%async_computation.12 | async-start | bytes 10616832 | tf_op jit(solution)/shard_map/all_gather | solution.py:246
  61.6 15.5 %copy-start.78 = (f32[384]{0:T(512)}, f32[384]{0:T(512)S(1)}, u32[]{:S(2)}) copy-start(f32[384]{0:T(512)S(1)} %rsqrt_bitcast_fusion) | copy-start | bytes 4612
  61.7 15.5 %copy-start.76 = (f32[384]{0:T(512)}, f32[384]{0:T(512)S(1)}, u32[]{:S(2)}) copy-start(f32[384]{0:T(512)S(1)} %rsqrt_bitcast_fusion.1) | copy-start | bytes 4612
  63.6 13.6 %copy-start.45 = (bf16[384,768]{1,0:T(8,128)(2,1)}, bf16[384,768]{1,0:T(8,128)(2,1)S(1)}, u32[]{:S(2)}) copy-start(bf16[384,768]{1,0:T(8,128)(2,1)S(1)} %get-tuple-element.980) | copy-start | bytes 1769476
  64.4 27.7 %copy-start.70 = (f32[128,8]{0,1:T(8,128)}, f32[128,8]{0,1:T(8,128)S(1)}, u32[]{:S(2)}) copy-start(f32[128,8]{0,1:T(8,128)S(1)} %get-tuple-element.1005) | copy-start | bytes 12292
  64.4 12.8 %copy-start.88 = (f32[2304]{0:T(1024)}, f32[2304]{0:T(1024)S(1)}, u32[]{:S(2)}) copy-start(f32[2304]{0:T(1024)S(1)} %convert_element_type.201) | copy-start | bytes 27652
  96.2 432.8 %all-gather.17.cloned.1.call-start = ((), (), s32[]{:S(2)}) async-start(), calls=%async_computation.14 | async-start | bytes 10616832 | tf_op jit(solution)/shard_map/all_gather | solution.py:246
  101.4 498.3 %all-gather.11.cloned.1.call-start = ((), (), s32[]{:S(2)}) async-start(), calls=%async_computation.10 | async-start | bytes 4866048 | tf_op jit(solution)/shard_map/all_gather | solution.py:148
  107.7 134.6 %all-to-all-start = ((bf16[8,3,128,1536]{2,3,1,0:T(8,128)(2,1)}), bf16[8,3,128,1536]{2,3,1,0:T(8,128)(2,1)}, u32[]{:S(2)}, u32[]{:S(2)}) async-start(bf16[8,3,128,1536]{2,3,1,0:T(8,128)(2,1)} %stack.4), calls=%async_computation | async-start | bytes 18874368 | tf_op jit(solution)/shard_map/all_to_all | solution.py:210
  112.8 498.4 %all-gather.13.cloned.1.call-start = ((), (), s32[]{:S(2)}) async-start(), calls=%async_computation.11 | async-start | bytes 4866048 | tf_op jit(solution)/shard_map/all_gather | solution.py:150
  114.3 127.9 %copy-start.13 = (bf16[3,128,1536]{1,2,0:T(8,128)(2,1)S(1)}, bf16[3,128,1536]{1,2,0:T(8,128)(2,1)}, u32[]{:S(2)}) copy-start(bf16[3,128,1536]{1,2,0:T(8,128)(2,1)} %pad_maximum_fusion.9) | copy-start | bytes 3538948
  116.7 136.3 %copy-start.47 = (bf16[384,768]{1,0:T(8,128)(2,1)}, bf16[384,768]{1,0:T(8,128)(2,1)S(1)}, u32[]{:S(2)}) copy-start(bf16[384,768]{1,0:T(8,128)(2,1)S(1)} %get-tuple-element.1018) | copy-start | bytes 1769476
  247.8 136.9 %all-to-all-start.1 = ((bf16[8,3,128,1536]{2,3,1,0:T(8,128)(2,1)}), bf16[8,3,128,1536]{2,3,1,0:T(8,128)(2,1)}, u32[]{:S(2)}, u32[]{:S(2)}) async-start(bf16[8,3,128,1536]{2,3,1,0:T(8,128)(2,1)} %stack.5), calls=%async_computation.1 | async-start | bytes 18874368 | tf_op jit(solution)/shard_map/all_to_all | solution.py:210
  253.0 402.3 %reduce-scatter.7.cloned.1.call-start = ((), (), s32[]{:S(2)}) async-start(), calls=%async_computation.13 | async-start | bytes 10616832 | tf_op jit(solution)/shard_map/reduce_scatter | solution.py:302
  464.4 224.1 %reduce-scatter.9.cloned.1.call-start = ((), (), s32[]{:S(2)}) async-start(), calls=%async_computation.15 | async-start | bytes 10616832 | tf_op jit(solution)/shard_map/reduce_scatter | solution.py:302
  597.2 204.4 %reduce-scatter.13.cloned.1.call-start = ((), (), s32[]{:S(2)}) async-start(), calls=%async_computation.17 | async-start | bytes 2433024 | tf_op jit(solution)/shard_map/reduce_scatter | solution.py:351
  599.7 7.7 copy-start.50
  611.1 324.5 %reduce-scatter.15.cloned.1.call-start = ((), (), s32[]{:S(2)}) async-start(), calls=%async_computation.18 | async-start | bytes 9732096 | tf_op jit(solution)/shard_map/reduce_scatter | solution.py:353
  618.4 8.8 slice-start.2
  627.1 15.5 %copy-start.25 = (bf16[384,3072]{1,0:T(8,128)(2,1)}, bf16[384,3072]{1,0:T(8,128)(2,1)S(1)}, u32[]{:S(2)}) copy-start(bf16[384,3072]{1,0:T(8,128)(2,1)S(1)} %get-tuple-element.1006) | copy-start | bytes 7077892
  638.0 439.3 %reduce-scatter.17.cloned.1.call-start = ((), (), s32[]{:S(2)}) async-start(), calls=%async_computation.19 | async-start | bytes 9732096 | tf_op jit(solution)/shard_map/reduce_scatter | solution.py:355
  647.9 554.0 %reduce-scatter.11.cloned.1.call-start = ((), (), s32[]{:S(2)}) async-start(), calls=%async_computation.16 | async-start | bytes 7299072 | tf_op jit(solution)/shard_map/reduce_scatter | solution.py:349
  698.5 39.0 %copy-start.15 = (f32[96,8,3,128]{3,1,2,0:T(8,128)}, f32[96,8,3,128]{3,1,2,0:T(8,128)S(1)}, u32[]{:S(2)}) copy-start(f32[96,8,3,128]{3,1,2,0:T(8,128)S(1)} %copy.273) | copy-start | bytes 3538948
  699.0 11.5 copy-start.17
  721.0 7.2 slice-start.4
  725.9 16.2 %copy-start.57 = (f32[384,768]{1,0:T(8,128)}, f32[384,768]{1,0:T(8,128)S(1)}, u32[]{:S(2)}) copy-start(f32[384,768]{1,0:T(8,128)S(1)} %fusion.91) | copy-start | bytes 3538948
  728.3 13.8 %copy-start.59 = (f32[384,768]{1,0:T(8,128)}, f32[384,768]{1,0:T(8,128)S(1)}, u32[]{:S(2)}) copy-start(f32[384,768]{1,0:T(8,128)S(1)} %fusion.87) | copy-start | bytes 3538948
  742.2 54.4 %copy-start.12 = (f32[3,128,768]{2,1,0:T(8,128)S(1)}, f32[3,128,768]{2,1,0:T(8,128)}, u32[]{:S(2)}) copy-start(f32[3,128,768]{2,1,0:T(8,128)} %copy-done.11) | copy-start | bytes 3538948
  787.7 414.2 %copy-start.96 = (f32[24]{0:T(128)}, f32[24]{0:T(128)S(1)}, u32[]{:S(2)}) copy-start(f32[24]{0:T(128)S(1)} %dynamic-slice.5) | copy-start | bytes 292
  (93 other events, 236.1 us)
Sparse Core Ops, SparseCore 0:
  10.9 62.6 all-gather.6
  76.5 54.0 all-gather.8
  132.4 131.1 all-gather.14
  265.4 135.6 all-gather.16
  403.8 61.3 all-gather.10
  468.0 61.9 all-gather.12
  533.4 74.9 reduce-scatter.6
  611.9 76.6 reduce-scatter.8
  694.4 99.5 reduce-scatter.12
  800.4 135.1 reduce-scatter.14
  942.1 135.1 reduce-scatter.16
  1083.3 118.4 reduce-scatter.10
